TPU v7x, 128 devices: a whole 4x4x4 slice. The times are simulated.
128 devices in a mesh: ctx: 32 (over y_lo, z, x), ch: 4 (over y_hi, core).
Axes of the slice: x: 4, y: 4 (y_hi: 2, y_lo: 2; y = y_hi * 2 + y_lo), z: 4, core: 2. Of those that a mesh axis runs over, the one named last changes fastest.
Arguments:
- query_gate: bfloat16 [8192, 4096], P('ctx', 'ch'), may hold values from -6 to 6
- gated_value: bfloat16 [8192, 4096], P('ctx', 'ch'), may hold values from -6 to 6
- long_filter: bfloat16 [8192, 4096], P(None, 'ch'), may hold values from -0.0625 to 0.0625
- out_weight: bfloat16 [4096, 4096], P('ch'), may hold values from -0.125 to 0.125
Outputs:
- output: bfloat16 [8192, 4096], P('ctx', 'ch')
All inputs are finite; a program needn't handle non-finite values.
Results may differ from a plain program's by a relative error of at most 0.019.
Values may be sent and summed in bfloat16 or wider, within the bound.
No kernel may reach another device: no remote copies, remote signals or barrier semaphores. Data moves between devices by JAX's collectives and lax.ppermute only.
A program may use at most 128 MiB of HBM per device.

v0:
```python
import math
import jax
import jax.numpy as jnp
from jax import lax
from jax.sharding import PartitionSpec as P

SPAN = 128


def dot_high(left, right):
    return jnp.dot(left, right, precision=lax.Precision.HIGHEST, preferred_element_type=jnp.float32)


def dot_plain(left, right):
    return jnp.dot(left, right, preferred_element_type=jnp.float32)


def make_tables():
    freq_int = jnp.arange(SPAN + 1, dtype=jnp.int32)[:, None]
    half_int = jnp.arange(SPAN, dtype=jnp.int32)[None, :]
    full_int = jnp.arange(2 * SPAN, dtype=jnp.int32)[None, :]
    half_phase = (freq_int * half_int % (2 * SPAN)).astype(jnp.float32) * (math.pi / SPAN)
    full_phase = (freq_int * full_int % (2 * SPAN)).astype(jnp.float32) * (math.pi / SPAN)
    parity = jnp.where(freq_int % 2 == 0, 1.0, -1.0).astype(jnp.float32)
    x_table = jnp.concatenate([jnp.cos(half_phase), -jnp.sin(half_phase)], 0).astype(jnp.bfloat16)
    filter_table = jnp.concatenate(
        [parity * jnp.cos(full_phase), -parity * jnp.sin(full_phase)], 0
    ).astype(jnp.bfloat16)
    weights = jnp.where((freq_int == 0) | (freq_int == SPAN), 1.0, 2.0).astype(jnp.float32)
    back_phase = half_phase.T
    inverse_table = jnp.concatenate(
        [weights.T * jnp.cos(back_phase), -weights.T * jnp.sin(back_phase)], 1
    ) / (2.0 * SPAN)
    return (x_table, filter_table, inverse_table)


def filter_spectrum(long_filter, filter_table, lag_block):
    first_row = jnp.maximum(lag_block * SPAN - SPAN, 0)
    window = lax.dynamic_slice_in_dim(long_filter, first_row, 2 * SPAN, 0)
    rolled = jnp.concatenate([jnp.zeros_like(window[:SPAN]), window[:SPAN]], 0)
    window = jnp.where(lag_block == 0, rolled, window)
    return dot_plain(filter_table, window)


def complex_times(filter_spec, source_spec, axis):
    freq_rows = SPAN + 1
    filt_real = lax.slice_in_dim(filter_spec, 0, freq_rows, axis=axis)
    filt_imag = lax.slice_in_dim(filter_spec, freq_rows, 2 * freq_rows, axis=axis)
    src_real = lax.slice_in_dim(source_spec, 0, freq_rows, axis=axis)
    src_imag = lax.slice_in_dim(source_spec, freq_rows, 2 * freq_rows, axis=axis)
    return jnp.concatenate(
        [filt_real * src_real - filt_imag * src_imag, filt_real * src_imag + filt_imag * src_real],
        axis,
    )


def block_number(position, axis_count):
    device_block = position // (2 * SPAN)
    second_half = position // SPAN % 2
    return jnp.where(second_half == 0, device_block, 2 * axis_count - 1 - device_block)


def per_device(query_gate, gated_value, long_filter, out_weight):
    x_table, filter_table, inverse_table = make_tables()
    axis_count = lax.axis_size("ctx")
    my_index = lax.axis_index("ctx")
    mine_high = 2 * axis_count - 1 - my_index
    channels = gated_value.shape[1]
    freq_rows = SPAN + 1

    def pair_term(lag_block, source_spec):
        return complex_times(filter_spectrum(long_filter, filter_table, lag_block), source_spec, 0)

    start_totals = jnp.zeros((2, 2 * freq_rows, channels), jnp.float32)
    shard_rows = lax.all_gather(gated_value, "ctx", axis=0, tiled=True)
    block_count = shard_rows.shape[0] // SPAN

    def one_block(block, totals):
        block_rows = lax.dynamic_slice_in_dim(shard_rows, block * SPAN, SPAN, 0)
        source = block_number(block * SPAN, axis_count)

        def include(inner):
            source_spec = dot_plain(x_table, block_rows)
            high_part = inner[1] + pair_term(mine_high - source, source_spec)

            def add_low(low_now):
                return low_now + pair_term(my_index - source, source_spec)

            def keep_low(low_now):
                return low_now

            low_part = lax.cond(source <= my_index, add_low, keep_low, inner[0])
            return jnp.stack([low_part, high_part])

        def skip_block(inner):
            return inner

        return lax.cond(source <= mine_high, include, skip_block, totals)

    totals = lax.fori_loop(0, block_count, one_block, start_totals)
    convolved = jnp.concatenate(
        [dot_high(inverse_table, totals[0]), dot_high(inverse_table, totals[1])], 0
    )
    gated_mix = (query_gate.astype(jnp.float32) * convolved).astype(jnp.bfloat16)
    partial_sum = jnp.dot(gated_mix, out_weight, preferred_element_type=jnp.float32)
    projected = lax.psum_scatter(
        partial_sum.astype(jnp.bfloat16), "ch", scatter_dimension=1, tiled=True
    )
    return projected


def solution(mesh):
    placed = (P("ctx", "ch"), P("ctx", "ch"), P(None, "ch"), P("ch", None))
    return jax.shard_map(
        per_device, mesh=mesh, in_specs=placed, out_specs=P("ctx", "ch"), check_vma=False
    )
```

profile of v0, /device:TPU:1, one launch (start us, length us, event | category | flops | bytes accessed | tf_op | source)
XLA Modules:
  0.0 738.9 jit_solution(10108354678242873776)
XLA Ops:
  10.8 189.1 %all-gather.2.cloned.1.call-done = bf16[8192,1024]{1,0:T(8,128)(2,1)} async-done(((bf16[256,1024]{1,0:T(8,128)(2,1)}), bf16[8192,1024]{1,0:T(8,128)(2,1)}) %all-gather.2.cloned.1.call-update) | async-done | bytes 16777232 | tf_op jit(solution)/shard_map/all_gather | solution.py:75
  201.5 478.4 %while.19 = (s32[]{:T(128)}, f32[2,258,1024]{2,1,0:T(8,128)}, s32[]{:T(128)}, s32[]{:T(128)}, bf16[8192,1024]{1,0:T(8,128)(2,1)}, /*index=5*/bf16[258,128]{1,0:T...) while((s32[]{:T(128)}, f32[2,258,1024]{2,1,0:T(8,128)}, ...), condition=%wide.region_5.6_spmd, body=%wide.region_0.5_spmd.sunk | while | flops 341860384 | bytes 25414548 | solution.py:100
  201.5 10.5 %conditional.3 = (f32[2,258,1024]{2,1,0:T(8,128)}) conditional(s32[]{:T(128)} %convert_element_type.75, f32[2,258,1024]{2,1,0:T(8,128)} %get-tuple-element.461, (s32[]{:T(128)}, s32[]{:T(128)}, f32[2,258,1024]{2,1,0:T(8,128)}, s32[]{:T(128)}, pred[]{:T(512)}, /*index=5*/bf16[8192,1024]{1,0:T(8,128)(2,1)}, bf16[258,128]{1,0:T(8,128)(2,1)}, ...), branch_computations={%region_1.1_spmd, %region_2.4_spmd} | conditional | flops 341860352 | bytes 25413872 | solution.py:98
  212.0 7.4 %conditional.3 = (f32[2,258,1024]{2,1,0:T(8,128)}) conditional(s32[]{:T(128)} %convert_element_type.75, f32[2,258,1024]{2,1,0:T(8,128)} %get-tuple-element.461, (s32[]{:T(128)}, s32[]{:T(128)}, f32[2,258,1024]{2,1,0:T(8,128)}, s32[]{:T(128)}, pred[]{:T(512)}, /*index=5*/bf16[8192,1024]{1,0:T(8,128)(2,1)}, bf16[258,128]{1,0:T(8,128)(2,1)}, ...), branch_computations={%region_1.1_spmd, %region_2.4_spmd} | conditional | flops 341860352 | bytes 25413872 | solution.py:98
  219.4 7.4 %conditional.3 = (f32[2,258,1024]{2,1,0:T(8,128)}) conditional(s32[]{:T(128)} %convert_element_type.75, f32[2,258,1024]{2,1,0:T(8,128)} %get-tuple-element.461, (s32[]{:T(128)}, s32[]{:T(128)}, f32[2,258,1024]{2,1,0:T(8,128)}, s32[]{:T(128)}, pred[]{:T(512)}, /*index=5*/bf16[8192,1024]{1,0:T(8,128)(2,1)}, bf16[258,128]{1,0:T(8,128)(2,1)}, ...), branch_computations={%region_1.1_spmd, %region_2.4_spmd} | conditional | flops 341860352 | bytes 25413872 | solution.py:98
  226.8 7.4 %conditional.3 = (f32[2,258,1024]{2,1,0:T(8,128)}) conditional(s32[]{:T(128)} %convert_element_type.75, f32[2,258,1024]{2,1,0:T(8,128)} %get-tuple-element.461, (s32[]{:T(128)}, s32[]{:T(128)}, f32[2,258,1024]{2,1,0:T(8,128)}, s32[]{:T(128)}, pred[]{:T(512)}, /*index=5*/bf16[8192,1024]{1,0:T(8,128)(2,1)}, bf16[258,128]{1,0:T(8,128)(2,1)}, ...), branch_computations={%region_1.1_spmd, %region_2.4_spmd} | conditional | flops 341860352 | bytes 25413872 | solution.py:98
  234.3 7.4 %conditional.3 = (f32[2,258,1024]{2,1,0:T(8,128)}) conditional(s32[]{:T(128)} %convert_element_type.75, f32[2,258,1024]{2,1,0:T(8,128)} %get-tuple-element.461, (s32[]{:T(128)}, s32[]{:T(128)}, f32[2,258,1024]{2,1,0:T(8,128)}, s32[]{:T(128)}, pred[]{:T(512)}, /*index=5*/bf16[8192,1024]{1,0:T(8,128)(2,1)}, bf16[258,128]{1,0:T(8,128)(2,1)}, ...), branch_computations={%region_1.1_spmd, %region_2.4_spmd} | conditional | flops 341860352 | bytes 25413872 | solution.py:98
  241.7 7.4 %conditional.3 = (f32[2,258,1024]{2,1,0:T(8,128)}) conditional(s32[]{:T(128)} %convert_element_type.75, f32[2,258,1024]{2,1,0:T(8,128)} %get-tuple-element.461, (s32[]{:T(128)}, s32[]{:T(128)}, f32[2,258,1024]{2,1,0:T(8,128)}, s32[]{:T(128)}, pred[]{:T(512)}, /*index=5*/bf16[8192,1024]{1,0:T(8,128)(2,1)}, bf16[258,128]{1,0:T(8,128)(2,1)}, ...), branch_computations={%region_1.1_spmd, %region_2.4_spmd} | conditional | flops 341860352 | bytes 25413872 | solution.py:98
  249.1 7.4 %conditional.3 = (f32[2,258,1024]{2,1,0:T(8,128)}) conditional(s32[]{:T(128)} %convert_element_type.75, f32[2,258,1024]{2,1,0:T(8,128)} %get-tuple-element.461, (s32[]{:T(128)}, s32[]{:T(128)}, f32[2,258,1024]{2,1,0:T(8,128)}, s32[]{:T(128)}, pred[]{:T(512)}, /*index=5*/bf16[8192,1024]{1,0:T(8,128)(2,1)}, bf16[258,128]{1,0:T(8,128)(2,1)}, ...), branch_computations={%region_1.1_spmd, %region_2.4_spmd} | conditional | flops 341860352 | bytes 25413872 | solution.py:98
  256.6 7.4 %conditional.3 = (f32[2,258,1024]{2,1,0:T(8,128)}) conditional(s32[]{:T(128)} %convert_element_type.75, f32[2,258,1024]{2,1,0:T(8,128)} %get-tuple-element.461, (s32[]{:T(128)}, s32[]{:T(128)}, f32[2,258,1024]{2,1,0:T(8,128)}, s32[]{:T(128)}, pred[]{:T(512)}, /*index=5*/bf16[8192,1024]{1,0:T(8,128)(2,1)}, bf16[258,128]{1,0:T(8,128)(2,1)}, ...), branch_computations={%region_1.1_spmd, %region_2.4_spmd} | conditional | flops 341860352 | bytes 25413872 | solution.py:98
  264.0 7.4 %conditional.3 = (f32[2,258,1024]{2,1,0:T(8,128)}) conditional(s32[]{:T(128)} %convert_element_type.75, f32[2,258,1024]{2,1,0:T(8,128)} %get-tuple-element.461, (s32[]{:T(128)}, s32[]{:T(128)}, f32[2,258,1024]{2,1,0:T(8,128)}, s32[]{:T(128)}, pred[]{:T(512)}, /*index=5*/bf16[8192,1024]{1,0:T(8,128)(2,1)}, bf16[258,128]{1,0:T(8,128)(2,1)}, ...), branch_computations={%region_1.1_spmd, %region_2.4_spmd} | conditional | flops 341860352 | bytes 25413872 | solution.py:98
  271.4 7.4 %conditional.3 = (f32[2,258,1024]{2,1,0:T(8,128)}) conditional(s32[]{:T(128)} %convert_element_type.75, f32[2,258,1024]{2,1,0:T(8,128)} %get-tuple-element.461, (s32[]{:T(128)}, s32[]{:T(128)}, f32[2,258,1024]{2,1,0:T(8,128)}, s32[]{:T(128)}, pred[]{:T(512)}, /*index=5*/bf16[8192,1024]{1,0:T(8,128)(2,1)}, bf16[258,128]{1,0:T(8,128)(2,1)}, ...), branch_computations={%region_1.1_spmd, %region_2.4_spmd} | conditional | flops 341860352 | bytes 25413872 | solution.py:98
  278.8 7.4 %conditional.3 = (f32[2,258,1024]{2,1,0:T(8,128)}) conditional(s32[]{:T(128)} %convert_element_type.75, f32[2,258,1024]{2,1,0:T(8,128)} %get-tuple-element.461, (s32[]{:T(128)}, s32[]{:T(128)}, f32[2,258,1024]{2,1,0:T(8,128)}, s32[]{:T(128)}, pred[]{:T(512)}, /*index=5*/bf16[8192,1024]{1,0:T(8,128)(2,1)}, bf16[258,128]{1,0:T(8,128)(2,1)}, ...), branch_computations={%region_1.1_spmd, %region_2.4_spmd} | conditional | flops 341860352 | bytes 25413872 | solution.py:98
  286.3 7.4 %conditional.3 = (f32[2,258,1024]{2,1,0:T(8,128)}) conditional(s32[]{:T(128)} %convert_element_type.75, f32[2,258,1024]{2,1,0:T(8,128)} %get-tuple-element.461, (s32[]{:T(128)}, s32[]{:T(128)}, f32[2,258,1024]{2,1,0:T(8,128)}, s32[]{:T(128)}, pred[]{:T(512)}, /*index=5*/bf16[8192,1024]{1,0:T(8,128)(2,1)}, bf16[258,128]{1,0:T(8,128)(2,1)}, ...), branch_computations={%region_1.1_spmd, %region_2.4_spmd} | conditional | flops 341860352 | bytes 25413872 | solution.py:98
  293.7 7.4 %conditional.3 = (f32[2,258,1024]{2,1,0:T(8,128)}) conditional(s32[]{:T(128)} %convert_element_type.75, f32[2,258,1024]{2,1,0:T(8,128)} %get-tuple-element.461, (s32[]{:T(128)}, s32[]{:T(128)}, f32[2,258,1024]{2,1,0:T(8,128)}, s32[]{:T(128)}, pred[]{:T(512)}, /*index=5*/bf16[8192,1024]{1,0:T(8,128)(2,1)}, bf16[258,128]{1,0:T(8,128)(2,1)}, ...), branch_computations={%region_1.1_spmd, %region_2.4_spmd} | conditional | flops 341860352 | bytes 25413872 | solution.py:98
  301.1 7.4 %conditional.3 = (f32[2,258,1024]{2,1,0:T(8,128)}) conditional(s32[]{:T(128)} %convert_element_type.75, f32[2,258,1024]{2,1,0:T(8,128)} %get-tuple-element.461, (s32[]{:T(128)}, s32[]{:T(128)}, f32[2,258,1024]{2,1,0:T(8,128)}, s32[]{:T(128)}, pred[]{:T(512)}, /*index=5*/bf16[8192,1024]{1,0:T(8,128)(2,1)}, bf16[258,128]{1,0:T(8,128)(2,1)}, ...), branch_computations={%region_1.1_spmd, %region_2.4_spmd} | conditional | flops 341860352 | bytes 25413872 | solution.py:98
  308.5 7.4 %conditional.3 = (f32[2,258,1024]{2,1,0:T(8,128)}) conditional(s32[]{:T(128)} %convert_element_type.75, f32[2,258,1024]{2,1,0:T(8,128)} %get-tuple-element.461, (s32[]{:T(128)}, s32[]{:T(128)}, f32[2,258,1024]{2,1,0:T(8,128)}, s32[]{:T(128)}, pred[]{:T(512)}, /*index=5*/bf16[8192,1024]{1,0:T(8,128)(2,1)}, bf16[258,128]{1,0:T(8,128)(2,1)}, ...), branch_computations={%region_1.1_spmd, %region_2.4_spmd} | conditional | flops 341860352 | bytes 25413872 | solution.py:98
  316.0 7.4 %conditional.3 = (f32[2,258,1024]{2,1,0:T(8,128)}) conditional(s32[]{:T(128)} %convert_element_type.75, f32[2,258,1024]{2,1,0:T(8,128)} %get-tuple-element.461, (s32[]{:T(128)}, s32[]{:T(128)}, f32[2,258,1024]{2,1,0:T(8,128)}, s32[]{:T(128)}, pred[]{:T(512)}, /*index=5*/bf16[8192,1024]{1,0:T(8,128)(2,1)}, bf16[258,128]{1,0:T(8,128)(2,1)}, ...), branch_computations={%region_1.1_spmd, %region_2.4_spmd} | conditional | flops 341860352 | bytes 25413872 | solution.py:98
  330.8 7.4 %conditional.3 = (f32[2,258,1024]{2,1,0:T(8,128)}) conditional(s32[]{:T(128)} %convert_element_type.75, f32[2,258,1024]{2,1,0:T(8,128)} %get-tuple-element.461, (s32[]{:T(128)}, s32[]{:T(128)}, f32[2,258,1024]{2,1,0:T(8,128)}, s32[]{:T(128)}, pred[]{:T(512)}, /*index=5*/bf16[8192,1024]{1,0:T(8,128)(2,1)}, bf16[258,128]{1,0:T(8,128)(2,1)}, ...), branch_computations={%region_1.1_spmd, %region_2.4_spmd} | conditional | flops 341860352 | bytes 25413872 | solution.py:98
  420.0 7.4 %conditional.3 = (f32[2,258,1024]{2,1,0:T(8,128)}) conditional(s32[]{:T(128)} %convert_element_type.75, f32[2,258,1024]{2,1,0:T(8,128)} %get-tuple-element.461, (s32[]{:T(128)}, s32[]{:T(128)}, f32[2,258,1024]{2,1,0:T(8,128)}, s32[]{:T(128)}, pred[]{:T(512)}, /*index=5*/bf16[8192,1024]{1,0:T(8,128)(2,1)}, bf16[258,128]{1,0:T(8,128)(2,1)}, ...), branch_computations={%region_1.1_spmd, %region_2.4_spmd} | conditional | flops 341860352 | bytes 25413872 | solution.py:98
  471.9 7.4 %conditional.3 = (f32[2,258,1024]{2,1,0:T(8,128)}) conditional(s32[]{:T(128)} %convert_element_type.75, f32[2,258,1024]{2,1,0:T(8,128)} %get-tuple-element.461, (s32[]{:T(128)}, s32[]{:T(128)}, f32[2,258,1024]{2,1,0:T(8,128)}, s32[]{:T(128)}, pred[]{:T(512)}, /*index=5*/bf16[8192,1024]{1,0:T(8,128)(2,1)}, bf16[258,128]{1,0:T(8,128)(2,1)}, ...), branch_computations={%region_1.1_spmd, %region_2.4_spmd} | conditional | flops 341860352 | bytes 25413872 | solution.py:98
  561.1 7.4 %conditional.3 = (f32[2,258,1024]{2,1,0:T(8,128)}) conditional(s32[]{:T(128)} %convert_element_type.75, f32[2,258,1024]{2,1,0:T(8,128)} %get-tuple-element.461, (s32[]{:T(128)}, s32[]{:T(128)}, f32[2,258,1024]{2,1,0:T(8,128)}, s32[]{:T(128)}, pred[]{:T(512)}, /*index=5*/bf16[8192,1024]{1,0:T(8,128)(2,1)}, bf16[258,128]{1,0:T(8,128)(2,1)}, ...), branch_computations={%region_1.1_spmd, %region_2.4_spmd} | conditional | flops 341860352 | bytes 25413872 | solution.py:98
  613.1 7.4 %conditional.3 = (f32[2,258,1024]{2,1,0:T(8,128)}) conditional(s32[]{:T(128)} %convert_element_type.75, f32[2,258,1024]{2,1,0:T(8,128)} %get-tuple-element.461, (s32[]{:T(128)}, s32[]{:T(128)}, f32[2,258,1024]{2,1,0:T(8,128)}, s32[]{:T(128)}, pred[]{:T(512)}, /*index=5*/bf16[8192,1024]{1,0:T(8,128)(2,1)}, bf16[258,128]{1,0:T(8,128)(2,1)}, ...), branch_computations={%region_1.1_spmd, %region_2.4_spmd} | conditional | flops 341860352 | bytes 25413872 | solution.py:98
  691.9 40.1 %reduce-scatter.2.cloned.1.call-done = bf16[256,1024]{1,0:T(8,128)(2,1)} async-done(((bf16[256,4096]{1,0:T(8,128)(2,1)}), bf16[256,1024]{1,0:T(8,128)(2,1)}) %reduce-scatter.2.cloned.1.call-update) | async-done | bytes 524304 | tf_op jit(solution)/shard_map/reduce_scatter | solution.py:106
  (514 shorter events, 815.2 us)
Async XLA Ops:
  6.5 193.3 %all-gather.2.cloned.1.call-start = ((), (), s32[]{:S(2)}) async-start(), calls=%async_computation.1 | async-start | bytes 17301504 | tf_op jit(solution)/shard_map/all_gather | solution.py:75
  7.3 724.8 %reduce-scatter.2.cloned.1.call-start = ((), (), s32[]{:S(2)}) async-start(), calls=%async_computation.2 | async-start | bytes 2621440 | tf_op jit(solution)/shard_map/reduce_scatter | solution.py:106
  679.9 4.9 copy-start
Sparse Core Ops, SparseCore 0:
  9.0 190.8 all-gather.1
  692.1 39.9 reduce-scatter.1
where the time goes:
time: 746 us; the launch traced here: 739 us
  other arithmetic  237 us (32%)
  waiting for transfers between devices  230 us (31%)
  matrix products  186 us (25%)
  local copies, waits for them, and re-layouts  68.5 us (9%)
  between operations  13.5 us (2%)
    all_gather x1, waiting for transfers between devices, per_device(): shard_rows = lax.all_gather(gated_value, 'ctx', axis=0, tiled=True)  189 us
    dot_general x129, matrix products, dot_plain(): return jnp.dot(left, right, preferred_element_type=jnp.float32)  174 us
    squeeze x64, other arithmetic, include(): low_part = lax.cond(source <= my_index, add_low, keep_low, inner[0])  120 us
    another operation x65, other arithmetic, include(): return jnp.stack([low_part, high_part])  97 us
    slice x65, local copies, waits for them, and re-layouts, filter_spectrum(): rolled = jnp.concatenate([jnp.zeros_like(window[:SPAN]), window[:SPAN]], 0)  66.8 us
    reduce_scatter x1, waiting for transfers between devices, per_device(): lax.psum_scatter(partial_sum.astype(jnp.bfloat16), 'ch', scatter_dimensio...  40.1 us
    concatenate x64, other arithmetic, complex_times(): jnp.concatenate([filt_real * src_real - filt_imag * src_imag, filt_real *...  15.8 us
  transfers between devices with their start and end apart: 2, of which 2 were waited for; matrix products, arithmetic and copies ran while one was open for 0% of the time, Pallas kernels for 0%

commit v1 on v0

--- a/solution.py
+++ b/solution.py
@@ -72,7 +72,9 @@
         return complex_times(filter_spectrum(long_filter, filter_table, lag_block), source_spec, 0)
 
     start_totals = jnp.zeros((2, 2 * freq_rows, channels), jnp.float32)
-    shard_rows = lax.all_gather(gated_value, "ctx", axis=0, tiled=True)
+    shard_rows = jnp.concatenate(
+        lax.all_to_all(jnp.stack([gated_value] * lax.axis_size("ctx"), 0), "ctx", 0, 0), axis=0
+    )
     block_count = shard_rows.shape[0] // SPAN
 
     def one_block(block, totals):

time: 746 us -> 823 us (1.10)
  waiting for transfers between devices: 230 us -> 292 us
  starting transfers between devices: 0.04 us -> 9.89 us
    all_to_all x0 -> x1, waiting for transfers between devices: none -> 256 us  [per_device(): lax.all_to_all(jnp.stack([gated_value] * lax.axis_size('ctx'), 0), 'ctx',...]
    all_gather x1 -> x0, waiting for transfers between devices: 189 us -> none  [per_device(): shard_rows = lax.all_gather(gated_value, 'ctx', axis=0, tiled=True)]
    all_to_all x0 -> x1, starting transfers between devices: none -> 9.85 us  [per_device(): lax.all_to_all(jnp.stack([gated_value] * lax.axis_size('ctx'), 0), 'ctx',...]
where the time goes in v1:
time: 823 us; the launch traced here: 816 us
  waiting for transfers between devices  292 us (35%)
  other arithmetic  236 us (29%)
  matrix products  186 us (23%)
  local copies, waits for them, and re-layouts  74.7 us (9%)
  between operations  13.5 us (2%)
  starting transfers between devices  9.89 us (1%)
    all_to_all x1, waiting for transfers between devices, per_device(): lax.all_to_all(jnp.stack([gated_value] * lax.axis_size('ctx'), 0), 'ctx',...  256 us
    dot_general x129, matrix products, dot_plain(): return jnp.dot(left, right, preferred_element_type=jnp.float32)  174 us
    squeeze x64, other arithmetic, include(): low_part = lax.cond(source <= my_index, add_low, keep_low, inner[0])  120 us
    another operation x65, other arithmetic, include(): return jnp.stack([low_part, high_part])  96.7 us
    slice x65, local copies, waits for them, and re-layouts, filter_spectrum(): rolled = jnp.concatenate([jnp.zeros_like(window[:SPAN]), window[:SPAN]], 0)  66.3 us
    reduce_scatter x1, waiting for transfers between devices, per_device(): lax.psum_scatter(partial_sum.astype(jnp.bfloat16), 'ch', scatter_dimensio...  35.8 us
  transfers between devices with their start and end apart: 2, of which 2 were waited for; matrix products, arithmetic and copies ran while one was open for 0% of the time, Pallas kernels for 0%

profile of v1, /device:TPU:1, one launch (start us, length us, event | category | flops | bytes accessed | tf_op | source)
XLA Modules:
  0.0 816.3 jit_solution(7366283177940545944)
XLA Ops:
  13.3 9.9 %all-to-all-start = ((bf16[32,256,1024]{2,1,0:T(8,128)(2,1)}), bf16[32,256,1024]{2,1,0:T(8,128)(2,1)}, u32[]{:S(2)}, u32[]{:S(2)}) async-start(bf16[32,256,1024]{2,1,0:T(8,128)(2,1)} %stack.14), calls=%async_computation | async-start | bytes 33554432 | tf_op jit(solution)/shard_map/all_to_all | solution.py:76
  26.7 256.3 %all-to-all-done = bf16[32,256,1024]{2,1,0:T(8,128)(2,1)} async-done(((bf16[32,256,1024]{2,1,0:T(8,128)(2,1)}), bf16[32,256,1024]{2,1,0:T(8,128)(2,1)}, u32[]{:S(2)}, u32[]{:S(2)}) %all-to-all-start) | async-done | bytes 16777248 | tf_op jit(solution)/shard_map/all_to_all | solution.py:76
  284.6 477.0 %while.19 = (s32[]{:T(128)}, f32[2,258,1024]{2,1,0:T(8,128)}, s32[]{:T(128)}, s32[]{:T(128)}, bf16[8192,1024]{1,0:T(8,128)(2,1)}, /*index=5*/bf16[258,128]{1,0:T...) while((s32[]{:T(128)}, f32[2,258,1024]{2,1,0:T(8,128)}, ...), condition=%wide.region_5.6_spmd, body=%wide.region_0.5_spmd.sunk | while | flops 341860384 | bytes 25414540 | solution.py:102
  284.6 10.5 %conditional.3 = (f32[2,258,1024]{2,1,0:T(8,128)}) conditional(s32[]{:T(128)} %convert_element_type.75, f32[2,258,1024]{2,1,0:T(8,128)} %get-tuple-element.461, (s32[]{:T(128)}, s32[]{:T(128)}, f32[2,258,1024]{2,1,0:T(8,128)}, s32[]{:T(128)}, pred[]{:T(512)}, /*index=5*/bf16[8192,1024]{1,0:T(8,128)(2,1)}, bf16[258,128]{1,0:T(8,128)(2,1)}, ...), branch_computations={%region_1.1_spmd, %region_2.4_spmd} | conditional | flops 341860352 | bytes 25413872 | solution.py:100
  295.1 7.4 conditional.3
  309.9 7.4 conditional.3
  332.2 7.4 conditional.3
  354.4 7.4 conditional.3
  376.6 7.4 conditional.3
  398.8 7.4 conditional.3
  421.0 7.4 conditional.3
  443.2 7.4 conditional.3
  465.4 7.4 conditional.3
  487.7 7.4 conditional.3
  509.9 7.4 conditional.3
  532.1 7.4 conditional.3
  554.3 7.4 conditional.3
  576.5 7.4 conditional.3
  598.7 7.4 conditional.3
  621.0 7.4 conditional.3
  643.2 7.4 conditional.3
  665.4 7.4 conditional.3
  687.6 7.4 conditional.3
  773.7 35.8 %reduce-scatter.2.cloned.1.call-done = bf16[256,1024]{1,0:T(8,128)(2,1)} async-done(((bf16[256,4096]{1,0:T(8,128)(2,1)}), bf16[256,1024]{1,0:T(8,128)(2,1)}) %reduce-scatter.2.cloned.1.call-update) | async-done | bytes 524304 | tf_op jit(solution)/shard_map/reduce_scatter | solution.py:108
  (514 shorter events, 825.9 us)
Async XLA Ops:
  13.3 269.7 %all-to-all-start = ((bf16[32,256,1024]{2,1,0:T(8,128)(2,1)}), bf16[32,256,1024]{2,1,0:T(8,128)(2,1)}, u32[]{:S(2)}, u32[]{:S(2)}) async-start(bf16[32,256,1024]{2,1,0:T(8,128)(2,1)} %stack.14), calls=%async_computation | async-start | bytes 33554432 | tf_op jit(solution)/shard_map/all_to_all | solution.py:76
  23.2 786.3 %reduce-scatter.2.cloned.1.call-start = ((), (), s32[]{:S(2)}) async-start(), calls=%async_computation.2 | async-start | bytes 2621440 | tf_op jit(solution)/shard_map/reduce_scatter | solution.py:108
  761.6 4.9 copy-start
Sparse Core Ops, SparseCore 0:
  773.8 35.6 reduce-scatter.1
